TPU v7x, 256 devices: a whole 4x4x8 slice. The times are simulated.
256 devices in a mesh: row: 8 (over x, core), col: 32 (over y, z).
Axes of the slice: x: 4, y: 4, z: 8, core: 2. Of those that a mesh axis runs over, the one named last changes fastest.
Arguments:
- matrix: float32 [16384, 16384], P('row', 'col'), as said below
- panel: float32 [16384, 256], P(('row', 'col')), may hold values from -0.046875 to 0.046875
- factor: float32 [256, 256], replicated, as said below
Outputs:
- updated: float32 [16384, 16384], P('row', 'col')
- correction: float32 [16384, 256], P(('row', 'col'))
Inputs may be any that keep to these rules, and one draw needn't show every extreme that they name: `matrix`: symmetric. `factor`: upper triangular with a positive diagonal.
All inputs are finite; a program needn't handle non-finite values.
Results may differ from a plain program's by a relative error of at most 0.000071.
Values sent between devices are 32-bit elements; how exact they have to be, the bound alone decides.
No kernel may reach another device: no remote copies, remote signals or barrier semaphores. Data moves between devices by JAX's collectives and lax.ppermute only.
A program may use at most 64 MiB of HBM per device.

v0:
```python
import jax
import jax.numpy as jnp
from jax import lax
from jax.sharding import PartitionSpec as P


def from_root(value, axis, source):
    kept = jnp.where(lax.axis_index(axis) == source, value, 0).astype(value.dtype)
    return lax.psum(kept, axis)


def mult(left, right):
    return jnp.dot(left, right, precision=lax.Precision.HIGHEST, preferred_element_type=jnp.float32)


def per_device(matrix, panel, factor):
    ncols = lax.axis_size("col")
    nrows = lax.axis_size("row")
    blocks = panel.shape[0]
    col_index = lax.axis_index("col")
    col_rows = blocks * nrows
    offset = col_index * nrows % ncols * blocks
    owner = col_index * nrows // ncols
    row_panel = lax.all_gather(panel, "col", axis=0, tiled=True)
    col_panel = from_root(lax.dynamic_slice_in_dim(row_panel, offset, col_rows, 0), "row", owner)
    product = lax.psum_scatter(mult(matrix, col_panel), "col", scatter_dimension=0, tiled=True)
    scaled = mult(product, factor)
    small = lax.psum(mult(panel.T, scaled), ("row", "col"))
    correction = scaled - 0.5 * mult(panel, mult(factor.T, small))
    row_corr = lax.all_gather(correction, "col", axis=0, tiled=True)
    col_corr = from_root(lax.dynamic_slice_in_dim(row_corr, offset, col_rows, 0), "row", owner)
    updated = matrix - mult(row_panel, col_corr.T) - mult(row_corr, col_panel.T)
    return (updated, correction)


def solution(mesh):
    in_specs = (P("row", "col"), P(("row", "col"), None), P())
    out_specs = (P("row", "col"), P(("row", "col"), None))
    return jax.shard_map(
        per_device, mesh=mesh, in_specs=in_specs, out_specs=out_specs, check_vma=False
    )
```

profile of v0, /device:TPU:8, one launch (start us, length us, event | category | flops | bytes accessed | tf_op | source)
XLA Modules:
  0.0 802.7 jit_solution(14840826598810947577)
XLA Ops:
  7.2 0.0 copy-start
  7.2 0.0 all-gather.3.cloned.1.call-start
  7.2 0.7 all-gather.3.cloned.1.call-update
  7.9 0.0 all-reduce.4.cloned.1.call-start
  8.0 82.3 %all-gather.3.cloned.1.call-done = f32[2048,256]{1,0:T(8,128)} async-done(((f32[64,256]{1,0:T(8,128)}), f32[2048,256]{1,0:T(8,128)}) %all-gather.3.cloned.1.call-update) | async-done | bytes 2097168 | tf_op jit(solution)/shard_map/all_gather | solution.py:24
  90.3 1.9 dynamic-slice_select_fusion.1
  92.1 0.0 all-reduce.4.cloned.1.call-update
  92.2 0.0 reduce-scatter.4.cloned.1.call-start
  92.2 65.1 %all-reduce.4.cloned.1.call-done = f32[512,256]{1,0:T(8,128)} async-done(((f32[512,256]{1,0:T(8,128)}), f32[512,256]{1,0:T(8,128)}) %all-reduce.4.cloned.1.call-update) | async-done | bytes 524304 | tf_op jit(solution)/shard_map/psum | solution.py:9
  157.3 8.7 %convolution_bitcast_fusion = f32[2048,256]{0,1:T(8,128)S(1)} fusion(f32[512,256]{1,0:T(8,128)} %all-reduce.4.cloned.1.call-done, f32[2048,512]{1,0:T(8,128)} %param.3), kind=kOutput, calls=%fused_computation.2 | convolution fusion | flops 3221225472 | bytes 6815744 | tf_op jit(solution)/shard_map/dot_general | solution.py:13
  166.0 0.0 copy-start.3
  166.0 1.8 copy.12
  167.8 0.0 reduce-scatter.4.cloned.1.call-update
  167.8 0.0 all-reduce.6.cloned.1.call-start
  167.9 214.8 %reduce-scatter.4.cloned.1.call-done = f32[64,256]{1,0:T(8,128)} async-done(((f32[2048,256]{1,0:T(8,128)}), f32[64,256]{1,0:T(8,128)}) %reduce-scatter.4.cloned.1.call-update) | async-done | bytes 65552
  382.7 1.1 fusion.3
  383.8 1.1 convolution_bitcast_fusion.1
  384.9 0.0 all-reduce.6.cloned.1.call-update
  384.9 0.0 all-gather.5.cloned.1.call-start
  385.0 252.9 %all-reduce.6.cloned.1.call-done = f32[256,256]{0,1:T(8,128)} async-done(((f32[256,256]{0,1:T(8,128)}), f32[256,256]{0,1:T(8,128)}) %all-reduce.6.cloned.1.call-update) | async-done | bytes 262160 | tf_op jit(solution)/shard_map/psum | solution.py:28
  637.9 1.3 fusion.4
  639.2 1.0 fusion.2
  640.3 0.0 all-gather.5.cloned.1.call-update
  640.3 0.0 all-reduce.8.cloned.1.call-start
  640.3 5.4 copy.8
  645.8 70.7 %all-gather.5.cloned.1.call-done = f32[2048,256]{1,0:T(8,128)} async-done(((f32[64,256]{1,0:T(8,128)}), f32[2048,256]{1,0:T(8,128)}) %all-gather.5.cloned.1.call-update) | async-done | bytes 2097168 | tf_op jit(solution)/shard_map/all_gather | solution.py:30
  716.5 1.9 dynamic-slice_select_fusion
  718.4 0.0 all-reduce.8.cloned.1.call-update
  718.4 6.9 fusion.5
  725.3 57.5 %all-reduce.8.cloned.1.call-done = f32[512,256]{1,0:T(8,128)} async-done(((f32[512,256]{1,0:T(8,128)}), f32[512,256]{1,0:T(8,128)}) %all-reduce.8.cloned.1.call-update) | async-done | bytes 524304 | tf_op jit(solution)/shard_map/psum | solution.py:9
  782.8 7.7 fusion
  790.5 5.3 copy.10
  (6 shorter events, 0.0 us)
Async XLA Ops:
  7.2 375.5 %copy-start = (f32[256,256]{1,0:T(8,128)S(1)}, f32[256,256]{1,0:T(8,128)}, u32[]{:S(2)}) copy-start(f32[256,256]{1,0:T(8,128)} %param.5) | copy-start | bytes 786436
  7.2 83.1 %all-gather.3.cloned.1.call-start = ((), (), s32[]{:S(2)}) async-start(), calls=%async_computation.1 | async-start | bytes 2162688 | tf_op jit(solution)/shard_map/all_gather | solution.py:24
  7.9 149.4 %all-reduce.4.cloned.1.call-start = ((), (), s32[]{:S(2)}) async-start(), calls=%async_computation.2 | async-start | bytes 1048576 | tf_op jit(solution)/shard_map/psum | solution.py:9
  92.2 290.5 %reduce-scatter.4.cloned.1.call-start = ((), (), s32[]{:S(2)}) async-start(), calls=%async_computation.6 | async-start | bytes 2162688
  166.0 217.8 %copy-start.3 = (f32[64,256]{1,0:T(8,128)S(1)}, f32[64,256]{1,0:T(8,128)}, u32[]{:S(2)}) copy-start(f32[64,256]{1,0:T(8,128)} %param.4) | copy-start | bytes 196612
  167.8 470.1 %all-reduce.6.cloned.1.call-start = ((), (), s32[]{:S(2)}) async-start(), calls=%async_computation.3 | async-start | bytes 524288 | tf_op jit(solution)/shard_map/psum | solution.py:28
  384.9 331.5 %all-gather.5.cloned.1.call-start = ((), (), s32[]{:S(2)}) async-start(), calls=%async_computation.4 | async-start | bytes 2162688 | tf_op jit(solution)/shard_map/all_gather | solution.py:30
  640.3 78.1 %copy-start.2 = (f32[512,256]{1,0:T(8,128)S(1)}, f32[512,256]{1,0:T(8,128)}, u32[]{:S(2)}) copy-start(f32[512,256]{1,0:T(8,128)} %all-reduce.4.cloned.1.call-done) | copy-start | bytes 1572868
  640.3 142.5 %all-reduce.8.cloned.1.call-start = ((), (), s32[]{:S(2)}) async-start(), calls=%async_computation.5 | async-start | bytes 1048576 | tf_op jit(solution)/shard_map/psum | solution.py:9
  645.8 137.0 %copy-start.1 = (f32[2048,256]{1,0:T(8,128)S(1)}, f32[2048,256]{1,0:T(8,128)}, u32[]{:S(2)}) copy-start(f32[2048,256]{1,0:T(8,128)} %all-gather.3.cloned.1.call-done) | copy-start | bytes 6291460
Sparse Core Ops, SparseCore 0:
  10.6 79.6 all-gather.2
  93.2 64.0 all-reduce.3
  168.0 214.6 reduce-scatter.3
  388.6 249.2 all-reduce.5
  640.9 75.5 all-gather.4
  718.7 64.0 all-reduce.7
where the time goes:
time: 803 us
  waiting for transfers between devices  744 us (93%)
  matrix products  27.9 us (3%)
  between operations  14.2 us (2%)
  local copies, waits for them, and re-layouts  12.6 us (2%)
    psum x1, waiting for transfers between devices, per_device(): small = lax.psum(mult(panel.T, scaled), ('row', 'col'))  253 us
    unnamed x7, waiting for transfers between devices  216 us
    psum x2, waiting for transfers between devices, from_root(): return lax.psum(kept, axis)  123 us
    all_gather x1, waiting for transfers between devices, per_device(): row_panel = lax.all_gather(panel, 'col', axis=0, tiled=True)  82.3 us
    all_gather x1, waiting for transfers between devices, per_device(): row_corr = lax.all_gather(correction, 'col', axis=0, tiled=True)  70.7 us
    dot_general x7, matrix products, mult(): jnp.dot(left, right, precision=lax.Precision.HIGHEST, preferred_element_t...  27.9 us
  transfers between devices with their start and end apart: 6, of which 6 were waited for; matrix products, arithmetic and copies ran while one was open for 2% of the time, Pallas kernels for 0%

commit v1 on v0

--- a/solution.py
+++ b/solution.py
@@ -25,7 +25,9 @@
     col_panel = from_root(lax.dynamic_slice_in_dim(row_panel, offset, col_rows, 0), "row", owner)
     product = lax.psum_scatter(mult(matrix, col_panel), "col", scatter_dimension=0, tiled=True)
     scaled = mult(product, factor)
-    small = lax.psum(mult(panel.T, scaled), ("row", "col"))
+    values = mult(panel.T, scaled)
+    after = jax.lax.psum(values, "col")
+    small = jax.lax.psum(after, "row")
     correction = scaled - 0.5 * mult(panel, mult(factor.T, small))
     row_corr = lax.all_gather(correction, "col", axis=0, tiled=True)
     col_corr = from_root(lax.dynamic_slice_in_dim(row_corr, offset, col_rows, 0), "row", owner)

time: 803 us -> 760 us (0.946)
  waiting for transfers between devices: 744 us -> 701 us
    psum x1 -> x2, waiting for transfers between devices: 253 us -> 209 us  [the longest x1 144 us: per_device(): after = jax.lax.psum(values, 'col')]
    unnamed x7 -> x8, waiting for transfers between devices: 216 us -> 216 us
  transfers between devices with their start and end apart: 6 -> 7, of which waited for: 6 -> 7; matrix products, arithmetic and copies ran while one was open for 2% -> 2% of each run, Pallas kernels for 0% -> 0%
where the time goes in v1:
time: 760 us
  waiting for transfers between devices  701 us (92%)
  matrix products  27.9 us (4%)
  between operations  14.2 us (2%)
  local copies, waits for them, and re-layouts  12.6 us (2%)
    unnamed x8, waiting for transfers between devices  216 us
    psum x1, waiting for transfers between devices, per_device(): after = jax.lax.psum(values, 'col')  144 us
    psum x2, waiting for transfers between devices, from_root(): return lax.psum(kept, axis)  123 us
    all_gather x1, waiting for transfers between devices, per_device(): row_panel = lax.all_gather(panel, 'col', axis=0, tiled=True)  82.3 us
    all_gather x1, waiting for transfers between devices, per_device(): row_corr = lax.all_gather(correction, 'col', axis=0, tiled=True)  71.4 us
    psum x1, waiting for transfers between devices, per_device(): small = jax.lax.psum(after, 'row')  65.1 us
    dot_general x7, matrix products, mult(): jnp.dot(left, right, precision=lax.Precision.HIGHEST, preferred_element_t...  27.9 us
  transfers between devices with their start and end apart: 7, of which 7 were waited for; matrix products, arithmetic and copies ran while one was open for 2% of the time, Pallas kernels for 0%

profile of v1, /device:TPU:8, one launch (start us, length us, event | category | flops | bytes accessed | tf_op | source)
XLA Modules:
  0.0 759.8 jit_solution(3837706875985428337)
XLA Ops:
  7.2 0.0 all-gather.3.cloned.1.call-start
  7.2 0.7 all-gather.3.cloned.1.call-update
  7.9 0.0 all-reduce.5.cloned.1.call-start
  8.0 82.3 %all-gather.3.cloned.1.call-done = f32[2048,256]{1,0:T(8,128)} async-done(((f32[64,256]{1,0:T(8,128)}), f32[2048,256]{1,0:T(8,128)}) %all-gather.3.cloned.1.call-update) | async-done | bytes 2097168 | tf_op jit(solution)/shard_map/all_gather | solution.py:24
  90.3 1.9 dynamic-slice_select_fusion.1
  92.1 0.0 all-reduce.5.cloned.1.call-update
  92.2 0.0 reduce-scatter.4.cloned.1.call-start
  92.2 65.1 %all-reduce.5.cloned.1.call-done = f32[512,256]{1,0:T(8,128)} async-done(((f32[512,256]{1,0:T(8,128)}), f32[512,256]{1,0:T(8,128)}) %all-reduce.5.cloned.1.call-update) | async-done | bytes 524304 | tf_op jit(solution)/shard_map/psum | solution.py:9
  157.3 8.7 %convolution_bitcast_fusion = f32[2048,256]{0,1:T(8,128)S(1)} fusion(f32[512,256]{1,0:T(8,128)} %all-reduce.5.cloned.1.call-done, f32[2048,512]{1,0:T(8,128)} %param.3), kind=kOutput, calls=%fused_computation.2 | convolution fusion | flops 3221225472 | bytes 6815744 | tf_op jit(solution)/shard_map/dot_general | solution.py:13
  166.0 1.8 copy.12
  167.8 0.0 reduce-scatter.4.cloned.1.call-update
  167.8 0.0 all-reduce.7.cloned.1.call-start
  167.9 214.8 %reduce-scatter.4.cloned.1.call-done = f32[64,256]{1,0:T(8,128)} async-done(((f32[2048,256]{1,0:T(8,128)}), f32[64,256]{1,0:T(8,128)}) %reduce-scatter.4.cloned.1.call-update) | async-done | bytes 65552
  382.7 1.1 fusion.3
  383.8 1.1 convolution_bitcast_fusion.1
  384.9 0.0 all-reduce.9.cloned.1.call-start
  385.0 143.8 %all-reduce.7.cloned.1.call-done = f32[256,256]{0,1:T(8,128)} async-done(((f32[256,256]{0,1:T(8,128)}), f32[256,256]{0,1:T(8,128)}) %all-reduce.7.cloned.1.call-update) | async-done | bytes 262160 | tf_op jit(solution)/shard_map/psum | solution.py:29
  528.8 0.0 all-reduce.9.cloned.1.call-update
  528.9 0.0 all-gather.5.cloned.1.call-start
  528.9 65.1 %all-reduce.9.cloned.1.call-done = f32[256,256]{0,1:T(8,128)} async-done(((f32[256,256]{0,1:T(8,128)}), f32[256,256]{0,1:T(8,128)}) %all-reduce.9.cloned.1.call-update) | async-done | bytes 262160 | tf_op jit(solution)/shard_map/psum | solution.py:30
  594.0 1.3 fusion.4
  595.4 1.0 fusion.2
  596.4 0.0 all-gather.5.cloned.1.call-update
  596.4 0.0 all-reduce.11.cloned.1.call-start
  596.5 5.4 copy.8
  601.9 71.4 %all-gather.5.cloned.1.call-done = f32[2048,256]{1,0:T(8,128)} async-done(((f32[64,256]{1,0:T(8,128)}), f32[2048,256]{1,0:T(8,128)}) %all-gather.5.cloned.1.call-update) | async-done | bytes 2097168 | tf_op jit(solution)/shard_map/all_gather | solution.py:32
  673.3 1.9 dynamic-slice_select_fusion
  675.2 0.0 all-reduce.11.cloned.1.call-update
  675.2 6.9 fusion.5
  682.2 57.7 %all-reduce.11.cloned.1.call-done = f32[512,256]{1,0:T(8,128)} async-done(((f32[512,256]{1,0:T(8,128)}), f32[512,256]{1,0:T(8,128)}) %all-reduce.11.cloned.1.call-update) | async-done | bytes 524304 | tf_op jit(solution)/shard_map/psum | solution.py:9
  739.9 7.7 %fusion = f32[2048,512]{0,1:T(8,128)} fusion(f32[2048,512]{0,1:T(8,128)} %fusion.5, f32[2048,512]{0,1:T(8,128)} %copy.8, f32[512,256]{1,0:T(8,128)} %all-reduce.11.cloned.1.call-done, f32[2048,256]{1,0:T(8,128)S(1)} %copy-done.1), kind=kOutput, calls=%fused_computation.1 | convolution fusion | flops 3223322624 | bytes 15204352 | tf_op jit(solution)/shard_map/dot_general | solution.py:13
  747.6 5.3 copy.10
  (9 shorter events, 0.0 us)
Async XLA Ops:
  7.2 375.5 %copy-start = (f32[256,256]{1,0:T(8,128)S(1)}, f32[256,256]{1,0:T(8,128)}, u32[]{:S(2)}) copy-start(f32[256,256]{1,0:T(8,128)} %param.5) | copy-start | bytes 786436
  7.2 83.1 %all-gather.3.cloned.1.call-start = ((), (), s32[]{:S(2)}) async-start(), calls=%async_computation.1 | async-start | bytes 2162688 | tf_op jit(solution)/shard_map/all_gather | solution.py:24
  7.9 149.4 %all-reduce.5.cloned.1.call-start = ((), (), s32[]{:S(2)}) async-start(), calls=%async_computation.2 | async-start | bytes 1048576 | tf_op jit(solution)/shard_map/psum | solution.py:9
  92.2 290.5 %reduce-scatter.4.cloned.1.call-start = ((), (), s32[]{:S(2)}) async-start(), calls=%async_computation.7 | async-start | bytes 2162688
  166.0 217.8 %copy-start.3 = (f32[64,256]{1,0:T(8,128)S(1)}, f32[64,256]{1,0:T(8,128)}, u32[]{:S(2)}) copy-start(f32[64,256]{1,0:T(8,128)} %param.4) | copy-start | bytes 196612
  167.8 361.0 %all-reduce.7.cloned.1.call-start = ((), (), s32[]{:S(2)}) async-start(), calls=%async_computation.3 | async-start | bytes 524288 | tf_op jit(solution)/shard_map/psum | solution.py:29
  384.9 209.1 %all-reduce.9.cloned.1.call-start = ((), (), s32[]{:S(2)}) async-start(), calls=%async_computation.4 | async-start | bytes 524288 | tf_op jit(solution)/shard_map/psum | solution.py:30
  528.9 144.5 %all-gather.5.cloned.1.call-start = ((), (), s32[]{:S(2)}) async-start(), calls=%async_computation.5 | async-start | bytes 2162688 | tf_op jit(solution)/shard_map/all_gather | solution.py:32
  596.4 78.8 %copy-start.2 = (f32[512,256]{1,0:T(8,128)S(1)}, f32[512,256]{1,0:T(8,128)}, u32[]{:S(2)}) copy-start(f32[512,256]{1,0:T(8,128)} %all-reduce.5.cloned.1.call-done) | copy-start | bytes 1572868
  596.4 143.5 %all-reduce.11.cloned.1.call-start = ((), (), s32[]{:S(2)}) async-start(), calls=%async_computation.6 | async-start | bytes 1048576 | tf_op jit(solution)/shard_map/psum | solution.py:9
  601.9 138.0 %copy-start.1 = (f32[2048,256]{1,0:T(8,128)S(1)}, f32[2048,256]{1,0:T(8,128)}, u32[]{:S(2)}) copy-start(f32[2048,256]{1,0:T(8,128)} %all-gather.3.cloned.1.call-done) | copy-start | bytes 6291460
Sparse Core Ops, SparseCore 0:
  10.6 79.6 all-gather.2
  93.2 64.0 all-reduce.4
  168.0 214.6 reduce-scatter.3
  386.6 142.2 all-reduce.6
  531.0 62.9 all-reduce.8
  597.4 75.8 all-gather.4
  675.8 64.0 all-reduce.10

commit v2 on v0

--- a/solution.py
+++ b/solution.py
@@ -2,11 +2,12 @@
 import jax.numpy as jnp
 from jax import lax
 from jax.sharding import PartitionSpec as P
+from jax.lax import all_gather
 
 
 def from_root(value, axis, source):
     kept = jnp.where(lax.axis_index(axis) == source, value, 0).astype(value.dtype)
-    return lax.psum(kept, axis)
+    return all_gather(kept, axis_name=axis).sum(axis=0)
 
 
 def mult(left, right):

time: 803 us -> 749 us (0.933)
  waiting for transfers between devices: 744 us -> 685 us
    psum x2 -> x0, waiting for transfers between devices: 123 us -> none  [from_root(): return lax.psum(kept, axis)]
    all_gather x0 -> x2, waiting for transfers between devices: none -> 56.1 us  [from_root(): return all_gather(kept, axis_name=axis).sum(axis=0)]
  transfers between devices with their start and end apart: 6 -> 6, of which waited for: 6 -> 6; matrix products, arithmetic and copies ran while one was open for 2% -> 1% of each run, Pallas kernels for 0% -> 0%
where the time goes in v2:
time: 749 us; the launch traced here: 747 us
  waiting for transfers between devices  685 us (91%)
  matrix products  25.8 us (3%)
  between operations  14.2 us (2%)
  local copies, waits for them, and re-layouts  12.7 us (2%)
  other arithmetic  8.79 us (1%)
    psum x1, waiting for transfers between devices, per_device(): small = lax.psum(mult(panel.T, scaled), ('row', 'col'))  254 us
    unnamed x7, waiting for transfers between devices  216 us
    all_gather x1, waiting for transfers between devices, per_device(): row_panel = lax.all_gather(panel, 'col', axis=0, tiled=True)  82.3 us
    all_gather x1, waiting for transfers between devices, per_device(): row_corr = lax.all_gather(correction, 'col', axis=0, tiled=True)  76.5 us
    all_gather x2, waiting for transfers between devices, from_root(): return all_gather(kept, axis_name=axis).sum(axis=0)  56.1 us
    dot_general x7, matrix products, mult(): jnp.dot(left, right, precision=lax.Precision.HIGHEST, preferred_element_t...  25.8 us
  transfers between devices with their start and end apart: 6, of which 6 were waited for; matrix products, arithmetic and copies ran while one was open for 1% of the time, Pallas kernels for 0%

profile of v2, /device:TPU:8, one launch (start us, length us, event | category | flops | bytes accessed | tf_op | source)
XLA Modules:
  0.0 747.0 jit_solution(338329593688970784)
XLA Ops:
  7.2 0.0 all-gather.7.cloned.1.call-start
  7.2 0.7 all-gather.7.cloned.1.call-update
  7.9 0.0 all-gather.11.cloned.1.call-start
  8.0 82.3 %all-gather.7.cloned.1.call-done = f32[2048,256]{1,0:T(8,128)} async-done(((f32[64,256]{1,0:T(8,128)}), f32[2048,256]{1,0:T(8,128)}) %all-gather.7.cloned.1.call-update) | async-done | bytes 2097168 | tf_op jit(solution)/shard_map/all_gather | solution.py:25
  90.3 1.9 dynamic-slice_select_fusion.1
  92.1 0.0 all-gather.11.cloned.1.call-update
  92.2 0.0 reduce-scatter.4.cloned.1.call-start
  92.2 33.6 %all-gather.11.cloned.1.call-done = f32[4096,256]{1,0:T(8,128)} async-done(((f32[512,256]{1,0:T(8,128)}), f32[4096,256]{1,0:T(8,128)}) %all-gather.11.cloned.1.call-update) | async-done | bytes 4194320 | tf_op jit(solution)/shard_map/all_gather | solution.py:10
  125.8 2.5 reduce_sum.18
  128.3 8.6 %convolution_bitcast_fusion = f32[2048,256]{0,1:T(8,128)S(1)} fusion(f32[512,256]{1,0:T(8,128)S(1)} %reduce_sum.18, f32[2048,512]{1,0:T(8,128)} %param.3), kind=kOutput, calls=%fused_computation.2 | convolution fusion | flops 3221225472 | bytes 6815744 | tf_op jit(solution)/shard_map/dot_general | solution.py:14
  136.9 1.8 copy.12
  138.8 0.0 reduce-scatter.4.cloned.1.call-update
  138.8 0.0 all-reduce.2.cloned.1.call-start
  138.8 215.5 %reduce-scatter.4.cloned.1.call-done = f32[64,256]{1,0:T(8,128)} async-done(((f32[2048,256]{1,0:T(8,128)}), f32[64,256]{1,0:T(8,128)}) %reduce-scatter.4.cloned.1.call-update) | async-done | bytes 65552
  354.4 1.1 fusion.3
  355.5 1.1 convolution_bitcast_fusion.1
  356.6 0.0 all-reduce.2.cloned.1.call-update
  356.6 0.0 all-gather.9.cloned.1.call-start
  356.7 254.0 %all-reduce.2.cloned.1.call-done = f32[256,256]{0,1:T(8,128)} async-done(((f32[256,256]{0,1:T(8,128)}), f32[256,256]{0,1:T(8,128)}) %all-reduce.2.cloned.1.call-update) | async-done | bytes 262160 | tf_op jit(solution)/shard_map/psum | solution.py:29
  610.7 1.3 fusion.4
  612.0 1.0 fusion.2
  613.0 0.0 all-gather.9.cloned.1.call-update
  613.0 0.0 all-gather.13.cloned.1.call-start
  613.1 76.5 %all-gather.9.cloned.1.call-done = f32[2048,256]{1,0:T(8,128)} async-done(((f32[64,256]{1,0:T(8,128)}), f32[2048,256]{1,0:T(8,128)}) %all-gather.9.cloned.1.call-update) | async-done | bytes 2097168 | tf_op jit(solution)/shard_map/all_gather | solution.py:31
  689.6 1.9 dynamic-slice_select_fusion
  691.5 0.0 all-gather.13.cloned.1.call-update
  691.5 5.5 copy.8
  697.0 5.1 fusion.5
  702.1 22.6 %all-gather.13.cloned.1.call-done = f32[4096,256]{1,0:T(8,128)} async-done(((f32[512,256]{1,0:T(8,128)}), f32[4096,256]{1,0:T(8,128)}) %all-gather.13.cloned.1.call-update) | async-done | bytes 4194320 | tf_op jit(solution)/shard_map/all_gather | solution.py:10
  724.7 2.5 reduce_sum.19
  727.2 7.6 %fusion = f32[2048,512]{0,1:T(8,128)} fusion(f32[2048,512]{0,1:T(8,128)} %fusion.5, f32[2048,512]{0,1:T(8,128)} %copy.8, f32[512,256]{1,0:T(8,128)S(1)} %reduce_sum.19, f32[2048,256]{1,0:T(8,128)S(1)} %copy-done.2), kind=kOutput, calls=%fused_computation.1 | convolution fusion | flops 3223322624 | bytes 15204352 | tf_op jit(solution)/shard_map/dot_general | solution.py:14
  734.8 5.3 copy.10
  (8 shorter events, 0.0 us)
Async XLA Ops:
  7.2 347.2 %copy-start = (f32[256,256]{1,0:T(8,128)S(1)}, f32[256,256]{1,0:T(8,128)}, u32[]{:S(2)}) copy-start(f32[256,256]{1,0:T(8,128)} %param.5) | copy-start | bytes 786436
  7.2 83.1 %all-gather.7.cloned.1.call-start = ((), (), s32[]{:S(2)}) async-start(), calls=%async_computation.1 | async-start | bytes 2162688 | tf_op jit(solution)/shard_map/all_gather | solution.py:25
  7.9 117.9 %all-gather.11.cloned.1.call-start = ((), (), s32[]{:S(2)}) async-start(), calls=%async_computation.4 | async-start | bytes 4718592 | tf_op jit(solution)/shard_map/all_gather | solution.py:10
  92.2 262.2 %reduce-scatter.4.cloned.1.call-start = ((), (), s32[]{:S(2)}) async-start(), calls=%async_computation.6 | async-start | bytes 2162688
  136.9 218.5 %copy-start.3 = (f32[64,256]{1,0:T(8,128)S(1)}, f32[64,256]{1,0:T(8,128)}, u32[]{:S(2)}) copy-start(f32[64,256]{1,0:T(8,128)} %param.4) | copy-start | bytes 196612
  138.8 471.9 %all-reduce.2.cloned.1.call-start = ((), (), s32[]{:S(2)}) async-start(), calls=%async_computation.2 | async-start | bytes 524288 | tf_op jit(solution)/shard_map/psum | solution.py:29
  356.6 332.9 %all-gather.9.cloned.1.call-start = ((), (), s32[]{:S(2)}) async-start(), calls=%async_computation.3 | async-start | bytes 2162688 | tf_op jit(solution)/shard_map/all_gather | solution.py:31
  613.0 111.6 %all-gather.13.cloned.1.call-start = ((), (), s32[]{:S(2)}) async-start(), calls=%async_computation.5 | async-start | bytes 4718592 | tf_op jit(solution)/shard_map/all_gather | solution.py:10
  691.5 5.5 copy-start.1
  702.1 25.1 %copy-start.2 = (f32[2048,256]{1,0:T(8,128)S(1)}, f32[2048,256]{1,0:T(8,128)}, u32[]{:S(2)}) copy-start(f32[2048,256]{1,0:T(8,128)} %all-gather.7.cloned.1.call-done) | copy-start | bytes 6291460
Sparse Core Ops, SparseCore 0:
  10.6 79.6 all-gather.6
  92.7 33.0 all-gather.10
  138.9 215.4 reduce-scatter.3
  361.2 249.4 all-reduce.1
  614.0 75.5 all-gather.8
  691.6 33.0 all-gather.12
